TPU v7x, 32 devices: a whole 2x2x4 slice. The times are simulated.
32 devices in a mesh: fsdp: 16 (over z, y, core), sp: 2 (over x).
Axes of the slice: x: 2, y: 2, z: 4, core: 2. Of those that a mesh axis runs over, the one named last changes fastest.
Arguments:
- latents: bfloat16 [32, 256, 768], P('fsdp', 'sp'), may hold values from -6 to 6
- condition: bfloat16 [32, 768], P('fsdp'), may hold values from -6 to 6
- cotangent: bfloat16 [32, 256, 768], P('fsdp', 'sp'), may hold values from -6 to 6
- w_ada: bfloat16 [768, 4608], P('fsdp'), may hold values from -0.21875 to 0.21875
- b_ada: bfloat16 [4608], P('fsdp'), may hold values from -3 to 3
- w_qkv: bfloat16 [768, 2304], P('fsdp'), may hold values from -0.21875 to 0.21875
- b_query: bfloat16 [768], P('fsdp'), may hold values from -3 to 3
- b_value: bfloat16 [768], P('fsdp'), may hold values from -3 to 3
- w_out: bfloat16 [768, 768], P('fsdp'), may hold values from -0.875 to 0.875
- b_out: bfloat16 [768], P('fsdp'), may hold values from -3 to 3
- w_up: bfloat16 [768, 3072], P('fsdp'), may hold values from -0.21875 to 0.21875
- b_up: bfloat16 [3072], P('fsdp'), may hold values from -3 to 3
- w_down: bfloat16 [3072, 768], P('fsdp'), may hold values from -0.109375 to 0.109375
- b_down: bfloat16 [768], P('fsdp'), may hold values from -3 to 3
Outputs:
- output: bfloat16 [32, 256, 768], P('fsdp', 'sp')
- grad_latents: float32 [32, 256, 768], P('fsdp', 'sp')
- grad_condition: float32 [32, 768], P('fsdp')
- grad_w_ada: float32 [768, 4608], P(('fsdp', 'sp'))
- grad_b_ada: float32 [4608], P(('fsdp', 'sp'))
- grad_w_qkv: float32 [768, 2304], P(('fsdp', 'sp'))
- grad_b_query: float32 [768], P(('fsdp', 'sp'))
- grad_b_value: float32 [768], P(('fsdp', 'sp'))
- grad_w_out: float32 [768, 768], P(('fsdp', 'sp'))
- grad_b_out: float32 [768], P(('fsdp', 'sp'))
- grad_w_up: float32 [768, 3072], P(('fsdp', 'sp'))
- grad_b_up: float32 [3072], P(('fsdp', 'sp'))
- grad_w_down: float32 [3072, 768], P(('fsdp', 'sp'))
- grad_b_down: float32 [768], P(('fsdp', 'sp'))
All inputs are finite; a program needn't handle non-finite values.
Results may differ from a plain program's by a relative error of at most 0.015.
The roundings to bfloat16 on the way count: a program that leaves them out, or rounds other values in their place, can miss the bound.
Values may be sent and summed in bfloat16 or wider, within the bound.
A program may use at most 256 MiB of HBM per device.

v0:
```python
import jax
import jax.numpy as jnp
from jax import lax
from jax.sharding import PartitionSpec as P

D = 768
H = 12
HD = 64
eps = 1e-06


def normalize(values):
    centered = values - jnp.mean(values, axis=-1, keepdims=True)
    inverse = lax.rsqrt(jnp.mean(centered * centered, axis=-1, keepdims=True) + eps)
    return (centered * inverse, inverse)


def norm_back(grad_in, normed, inverse):
    return inverse * (
        grad_in
        - jnp.mean(grad_in, axis=-1, keepdims=True)
        - normed * jnp.mean(grad_in * normed, axis=-1, keepdims=True)
    )


def gelu_tanh(values):
    return jax.nn.gelu(values, approximate=True)


def silu_back(values, grad_out):
    return jax.vjp(jax.nn.silu, values)[1](grad_out)[0]


def gelu_back(values, grad_out):
    return jax.vjp(gelu_tanh, values)[1](grad_out)[0]


LANES = 2048


def body(
    latents,
    condition,
    cotangent,
    w_ada,
    b_ada,
    w_qkv,
    b_query,
    b_value,
    w_out,
    b_out,
    w_up,
    b_up,
    w_down,
    b_down,
):
    f32 = jnp.float32
    bf16 = jnp.bfloat16
    fsdp_count = lax.axis_size("fsdp")
    sp_count = lax.axis_size("sp")
    owners = fsdp_count * sp_count
    fsdp_index = lax.axis_index("fsdp")
    sp_index = lax.axis_index("sp")
    owner_index = fsdp_index * sp_count + sp_index
    pair_latents = latents.shape[0]
    own_latents = pair_latents // sp_count
    latent_total = pair_latents * fsdp_count
    tokens_all = latents.shape[1] * sp_count
    scale_factor = HD ** (-0.5)
    small = [condition.reshape(-1), b_ada, b_query, b_value, b_out, b_up, b_down]
    width = sum((part.size for part in small))
    padded = -(-width // LANES) * LANES
    small.append(jnp.zeros((padded - width,), bf16))
    small_all = lax.all_gather(
        jnp.concatenate(small).reshape(1, padded // 128, 128), "fsdp", axis=0, tiled=True
    ).reshape(fsdp_count, padded)
    pieces = []
    start = 0
    for part in small[:-1]:
        pieces.append(small_all[:, start : start + part.size].reshape(-1))
        start = start + part.size
    cond_all, ada_bias, query_bias, value_bias, out_bias, up_bias, down_bias = pieces
    cond_all = cond_all.reshape(latent_total, D).astype(f32)
    silu_all = jax.nn.silu(cond_all)
    inputs = lax.all_to_all(latents, "sp", split_axis=0, concat_axis=1, tiled=True).astype(f32)
    grad_out = lax.all_to_all(cotangent, "sp", split_axis=0, concat_axis=1, tiled=True).astype(f32)
    ada_rows = w_ada.shape[0]
    silu_mine = lax.dynamic_index_in_dim(
        silu_all.astype(bf16).reshape(fsdp_count, sp_count, own_latents, D), sp_index, 1, False
    )
    silu_mine = lax.dynamic_index_in_dim(
        silu_mine.reshape(fsdp_count * own_latents, fsdp_count, ada_rows), fsdp_index, 1, False
    )
    mod_part = jnp.dot(silu_mine, w_ada, preferred_element_type=f32)
    mod_part = lax.all_to_all(
        mod_part.reshape(fsdp_count, own_latents * 6 * D),
        "fsdp",
        split_axis=0,
        concat_axis=0,
        tiled=True,
    )
    modulate = jnp.sum(mod_part, axis=0).reshape(own_latents, 6 * D) + ada_bias.astype(f32)
    mod_parts = modulate.reshape(own_latents, 6, 1, D)
    shift_one, scale_one, gate_one = (mod_parts[:, 0], mod_parts[:, 1], mod_parts[:, 2])
    shift_two, scale_two, gate_two = (mod_parts[:, 3], mod_parts[:, 4], mod_parts[:, 5])
    qkv_full = lax.all_gather(w_qkv, "fsdp", axis=0, tiled=True)
    out_full = lax.all_gather(w_out, "fsdp", axis=0, tiled=True)
    up_full = lax.all_gather(w_up, "fsdp", axis=0, tiled=True)
    down_full = lax.all_gather(w_down, "fsdp", axis=0, tiled=True)
    normed_one, inverse_one = normalize(inputs)
    attn_in = (normed_one * (1.0 + scale_one) + shift_one).astype(bf16)
    qkv_bias = jnp.concatenate([query_bias, jnp.zeros_like(query_bias), value_bias]).astype(f32)
    projected = (
        jnp.einsum("btd,de->bte", attn_in, qkv_full, preferred_element_type=f32) + qkv_bias
    ).astype(bf16)
    heads = projected.reshape(own_latents, tokens_all, 3, H, HD).transpose(2, 0, 3, 1, 4)
    queries, key_heads, value_heads = (heads[0], heads[1], heads[2])
    scores = (
        jnp.einsum("bhqd,bhkd->bhqk", queries, key_heads, preferred_element_type=f32) * scale_factor
    )
    log_total = jnp.log(jnp.sum(jnp.exp(scores), axis=-1, keepdims=True))
    soft_float = jnp.exp(scores - log_total)
    soft_half = soft_float.astype(bf16)
    mixed = jnp.einsum(
        "bhqk,bhkd->bhqd", soft_half, value_heads, preferred_element_type=f32
    ).astype(bf16)
    mixed_tokens = mixed.transpose(0, 2, 1, 3).reshape(own_latents, tokens_all, D)
    attn_proj = jnp.einsum(
        "btd,de->bte", mixed_tokens, out_full, preferred_element_type=f32
    ) + out_bias.astype(f32)
    residual = inputs + gate_one * attn_proj
    normed_two, inverse_two = normalize(residual)
    mlp_in = (normed_two * (1.0 + scale_two) + shift_two).astype(bf16)
    up_value = jnp.einsum(
        "btd,df->btf", mlp_in, up_full, preferred_element_type=f32
    ) + up_bias.astype(f32)
    activated = gelu_tanh(up_value).astype(bf16)
    down_value = jnp.einsum(
        "btf,fd->btd", activated, down_full, preferred_element_type=f32
    ) + down_bias.astype(f32)
    output = (residual + gate_two * down_value).astype(bf16)
    output = lax.all_to_all(output, "sp", split_axis=1, concat_axis=0, tiled=True)
    grad_gate_two = jnp.sum(grad_out * down_value, axis=1)
    grad_down = (grad_out * gate_two).astype(bf16)
    gw_down = jnp.einsum("btf,btd->fd", activated, grad_down, preferred_element_type=f32)
    gb_down = jnp.sum(grad_down.astype(f32), axis=(0, 1))
    grad_act = jnp.einsum("btd,fd->btf", grad_down, down_full, preferred_element_type=f32)
    grad_up = gelu_back(up_value, grad_act).astype(bf16)
    gw_up = jnp.einsum("btd,btf->df", mlp_in, grad_up, preferred_element_type=f32)
    gb_up = jnp.sum(grad_up.astype(f32), axis=(0, 1))
    grad_mlp = jnp.einsum("btf,df->btd", grad_up, up_full, preferred_element_type=f32)
    grad_scale_two = jnp.sum(grad_mlp * normed_two, axis=1)
    grad_shift_two = jnp.sum(grad_mlp, axis=1)
    grad_resid = grad_out + norm_back(grad_mlp * (1.0 + scale_two), normed_two, inverse_two)
    grad_gate_one = jnp.sum(grad_resid * attn_proj, axis=1)
    grad_proj = (grad_resid * gate_one).astype(bf16)
    gw_out = jnp.einsum("btd,bte->de", mixed_tokens, grad_proj, preferred_element_type=f32)
    gb_out = jnp.sum(grad_proj.astype(f32), axis=(0, 1))
    grad_mixed = jnp.einsum("bte,de->btd", grad_proj, out_full, preferred_element_type=f32).astype(
        bf16
    )
    grad_heads = grad_mixed.reshape(own_latents, tokens_all, H, HD).transpose(0, 2, 1, 3)
    grad_soft = jnp.einsum("bhqd,bhkd->bhqk", grad_heads, value_heads, preferred_element_type=f32)
    delta_sum = jnp.sum(soft_float * grad_soft, axis=-1, keepdims=True)
    grad_scores = (soft_float * (grad_soft - delta_sum)).astype(bf16)
    grad_queries = (
        jnp.einsum("bhqk,bhkd->bhqd", grad_scores, key_heads, preferred_element_type=f32)
        * scale_factor
    ).astype(bf16)
    grad_keys = (
        jnp.einsum("bhqk,bhqd->bhkd", grad_scores, queries, preferred_element_type=f32)
        * scale_factor
    ).astype(bf16)
    grad_values = jnp.einsum(
        "bhqk,bhqd->bhkd", soft_half, grad_heads, preferred_element_type=f32
    ).astype(bf16)
    grad_tokens = (
        jnp.stack([grad_queries, grad_keys, grad_values], axis=0)
        .transpose(1, 3, 0, 2, 4)
        .reshape(own_latents, tokens_all, 3 * D)
    )
    gw_qkv = jnp.einsum("btd,bte->de", attn_in, grad_tokens, preferred_element_type=f32)
    grad_tok_float = grad_tokens.astype(f32)
    gb_query = jnp.sum(grad_tok_float[:, :, :D], axis=(0, 1))
    gb_value = jnp.sum(grad_tok_float[:, :, 2 * D :], axis=(0, 1))
    grad_attn_in = jnp.einsum("bte,de->btd", grad_tokens, qkv_full, preferred_element_type=f32)
    grad_scale_one = jnp.sum(grad_attn_in * normed_one, axis=1)
    grad_shift_one = jnp.sum(grad_attn_in, axis=1)
    grad_latents = grad_resid + norm_back(grad_attn_in * (1.0 + scale_one), normed_one, inverse_one)
    grad_latents = lax.all_to_all(grad_latents, "sp", split_axis=1, concat_axis=0, tiled=True)
    grad_mod = jnp.concatenate(
        [
            grad_shift_one,
            grad_scale_one,
            grad_gate_one,
            grad_shift_two,
            grad_scale_two,
            grad_gate_two,
        ],
        axis=1,
    )
    grad_mod = lax.all_to_all(
        jnp.broadcast_to(grad_mod[None], (owners, own_latents, 6 * D)),
        ("fsdp", "sp"),
        split_axis=0,
        concat_axis=0,
        tiled=True,
    ).reshape(latent_total, 6 * D)
    rows = D // owners
    biases = (gb_query, gb_value, gb_out, gb_up, gb_down)
    bias_rows = jnp.concatenate([part.reshape(owners, -1) for part in biases], axis=1)
    bias_width = bias_rows.shape[1]
    bias_lanes = -(-bias_width // (rows * 128)) * 128
    bias_rows = jnp.pad(bias_rows, ((0, 0), (0, rows * bias_lanes - bias_width)))
    stack = down_full.shape[0] // D
    gw_down = (
        gw_down.astype(bf16)
        .reshape(owners, stack, rows, D)
        .transpose(0, 2, 1, 3)
        .reshape(D, stack * D)
    )
    packed = jnp.concatenate(
        [
            gw_down,
            gw_up.astype(bf16),
            gw_qkv.astype(bf16),
            gw_out.astype(bf16),
            bias_rows.astype(bf16).reshape(D, bias_lanes),
        ],
        axis=1,
    )
    owned = lax.psum_scatter(packed, ("fsdp", "sp"), scatter_dimension=0, tiled=True).astype(f32)
    own_weights = []
    start = 0
    for width in (stack * D, up_full.shape[1], 3 * D, D, bias_lanes):
        own_weights.append(owned[:, start : start + width])
        start = start + width
    own_down, own_up, own_qkv, own_out, bias_sums = own_weights
    own_down = own_down.reshape(rows, stack, D).transpose(1, 0, 2).reshape(stack * rows, D)
    bias_sums = bias_sums.reshape(-1)
    own_bias = []
    start = 0
    for part in biases:
        width = part.size // owners
        own_bias.append(bias_sums[start : start + width])
        start = start + width
    own_gb_query, own_gb_value, own_gb_out, own_gb_up, own_gb_down = own_bias
    silu_rows = lax.dynamic_index_in_dim(
        silu_all.reshape(latent_total, owners, D // owners), owner_index, 1, False
    )
    own_ada = jnp.dot(silu_rows.T, grad_mod, precision=lax.Precision.HIGHEST)
    own_gb_ada = lax.dynamic_index_in_dim(
        jnp.sum(grad_mod, axis=0).reshape(owners, -1), owner_index, 0, False
    )
    grad_silu = jnp.dot(grad_mod.astype(bf16), w_ada.T, preferred_element_type=f32)
    grad_silu = lax.all_to_all(
        grad_silu.reshape(fsdp_count, pair_latents * ada_rows),
        "fsdp",
        split_axis=0,
        concat_axis=0,
        tiled=True,
    )
    grad_silu = (
        grad_silu.reshape(fsdp_count, pair_latents, ada_rows)
        .transpose(1, 0, 2)
        .reshape(pair_latents, D)
    )
    grad_condition = silu_back(condition.astype(f32), grad_silu)
    return (
        output,
        grad_latents,
        grad_condition,
        own_ada,
        own_gb_ada,
        own_qkv,
        own_gb_query,
        own_gb_value,
        own_out,
        own_gb_out,
        own_up,
        own_gb_up,
        own_down,
        own_gb_down,
    )


def solution(mesh):
    in_specs = (
        P("fsdp", "sp", None),
        P("fsdp", None),
        P("fsdp", "sp", None),
        P("fsdp", None),
        P("fsdp"),
        P("fsdp", None),
        P("fsdp"),
        P("fsdp"),
        P("fsdp", None),
        P("fsdp"),
        P("fsdp", None),
        P("fsdp"),
        P("fsdp", None),
        P("fsdp"),
    )
    out_specs = (
        P("fsdp", "sp", None),
        P("fsdp", "sp", None),
        P("fsdp", None),
        P(("fsdp", "sp"), None),
        P(("fsdp", "sp")),
        P(("fsdp", "sp"), None),
        P(("fsdp", "sp")),
        P(("fsdp", "sp")),
        P(("fsdp", "sp"), None),
        P(("fsdp", "sp")),
        P(("fsdp", "sp"), None),
        P(("fsdp", "sp")),
        P(("fsdp", "sp"), None),
        P(("fsdp", "sp")),
    )
    return jax.shard_map(body, mesh=mesh, in_specs=in_specs, out_specs=out_specs, check_vma=False)
```

profile of v0, /device:TPU:0, one launch (start us, length us, event | category | flops | bytes accessed | tf_op | source)
XLA Modules:
  0.0 443.4 jit_solution(5523221434767197551)
XLA Ops:
  8.0 0.7 all-gather.7.cloned.1.call-update
  10.0 4.2 all-to-all-start
  14.2 0.7 reshape.728
  14.9 4.1 concatenate.24
  19.1 22.7 %all_gather.15 = bf16[16,32,128]{2,1,0:T(8,128)(2,1)S(1)} all-gather(bf16[1,32,128]{2,1,0:T(8,128)(2,1)S(1)} %bitcast.188), channel_id=1, replica_groups=mesh['fsdp'=16,'sp'=2] {'fsdp'}, dimensions={0}, use_global_device_ids=true | all-gather | bytes 139264 | tf_op jit(solution)/shard_map/all_gather | solution.py:74
  42.6 1.0 copy.104
  43.7 3.5 all-to-all-start.1
  48.0 13.7 %all-to-all-done.1 = f32[16,1,4608]{2,1,0:T(1,128)S(1)} async-done(((f32[16,1,4608]{2,1,0:T(1,128)}), f32[16,1,4608]{2,1,0:T(1,128)S(1)}, u32[]{:S(2)}, u32[]{:S(2)}) %all-to-all-start.1) | async-done | bytes 294944 | tf_op jit(solution)/shard_map/all_to_all | solution.py:95
  61.7 3.8 all-to-all-start.3
  65.8 6.4 %all-to-all-done.3 = bf16[2,128,768]{2,1,0:T(8,128)(2,1)S(1)} async-done(((bf16[2,128,768]{2,1,0:T(8,128)(2,1)}), bf16[2,128,768]{2,1,0:T(8,128)(2,1)S(1)}, u32[]{:S(2)}, u32[]{:S(2)}) %all-to-all-start.3) | async-done | bytes 393248 | tf_op jit(solution)/shard_map/all_to_all | solution.py:86
  72.4 0.8 fusion.24
  73.5 1.0 fusion.43
  74.5 4.1 fusion.3
  78.6 1.6 copy.105
  80.2 2.4 fusion.60
  82.6 4.9 %convolution_convert_fusion.4 = bf16[12,256,64]{1,2,0:T(8,128)(2,1)} fusion(f32[12,256,256]{1,2,0:T(8,128)} %fusion.60, bf16[3,1,12,256,64]{3,4,2,1,0:T(8,128)(2,1)S(1)} %bitcast.160), kind=kOutput, calls=%fused_computation.34 | convolution fusion | flops 104008960 | bytes 7077888 | tf_op jit(solution)/shard_map/bhqk,bhkd->bhqd/dot_general | solution.py:124
  87.4 17.1 %all-gather.7.cloned.1.call-done = bf16[768,768]{1,0:T(8,128)(2,1)} async-done(((bf16[48,768]{1,0:T(8,128)(2,1)}), bf16[768,768]{1,0:T(8,128)(2,1)}) %all-gather.7.cloned.1.call-update) | async-done | bytes 1179664 | tf_op jit(solution)/shard_map/all_gather | solution.py:107
  104.6 2.8 fusion.83
  107.6 51.3 %all-gather.11.cloned.1.call-done = bf16[3072,768]{1,0:T(8,128)(2,1)} async-done(((bf16[192,768]{1,0:T(8,128)(2,1)}), bf16[3072,768]{1,0:T(8,128)(2,1)}) %all-gather.11.cloned.1.call-update) | async-done | bytes 4718608 | tf_op jit(solution)/shard_map/all_gather | solution.py:109
  158.9 5.6 %fusion.86 = f32[256,3072]{1,0:T(8,128)} fusion(bf16[256,768]{1,0:T(8,128)(2,1)} %fusion.24, bf16[3072,768]{1,0:T(8,128)(2,1)} %all-gather.11.cloned.1.call-done), kind=kOutput, calls=%fused_computation.159 | convolution fusion | flops 1207959552 | bytes 8257536 | tf_op jit(solution)/shard_map/btd,fd->btf/dot_general | solution.py:147
  164.5 48.2 %all-gather.9.cloned.1.call-done = bf16[768,3072]{1,0:T(8,128)(2,1)} async-done(((bf16[48,3072]{1,0:T(8,128)(2,1)}), bf16[768,3072]{1,0:T(8,128)(2,1)}) %all-gather.9.cloned.1.call-update) | async-done | bytes 4718608 | tf_op jit(solution)/shard_map/all_gather | solution.py:108
  212.7 7.0 %fusion.80 = (bf16[3072]{0:T(1024)(128)(2,1)S(1)}, bf16[256,3072]{1,0:T(8,128)(2,1)S(1)}, f32[256,3072]{1,0:T(8,128)S(1)}) fusion(f32[256,3072]{1,0:T(8,128)} %fusion.86, f32[3072]{0:T(1024)S(1)} %reshape.760, bf16[768,3072]{1,0:T(8,128)(2,1)} %all-gather.9.cloned.1.call-done, f32[256,768]{1,0:T(8,128)S(1)} %get-tuple-element.36, ...), kind=kOutput, calls=%fused_computation.153 | convolution fusion | flops 1226241024 | bytes 13395968 | tf_op jit(solution)/shard_map/btd,df->btf/dot_general | solution.py:134
  219.8 1.4 fusion.87
  221.2 0.9 copy-done.19
  222.1 1.7 copy-done.2
  223.8 2.9 fusion.25
  226.7 1.3 fusion.82
  228.0 0.8 copy-done.5
  229.3 0.9 copy.109
  230.2 5.0 %fusion.20 = bf16[1,1,12,256,64]{3,4,2,1,0:T(8,128)(2,1)} fusion(bf16[12,256,64]{1,2,0:T(8,128)(2,1)} %bitcast.174, f32[12,256,256]{1,2,0:T(8,128)} %fusion.60), kind=kOutput, calls=%fused_computation.39 | convolution fusion | flops 104008960 | bytes 3932160 | tf_op jit(solution)/shard_map/bhqk,bhqd->bhkd/dot_general | solution.py:174
  235.8 1.3 copy-done.1
  237.1 2.9 multiply_reduce_fusion
  240.6 1.4 fusion.22
  241.9 1.1 fusion.21
  243.1 4.4 convolution_convert_fusion.2
  247.7 1.2 pad_maximum_fusion
  249.8 4.7 %copy.117 = bf16[32,24,4,768]{3,2,1,0:T(4,128)(2,1)S(1)} copy(bf16[32,24,4,768]{3,1,2,0:T(8,128)(2,1)} %bitcast.167) | data formatting | bytes 9437184 | tf_op jit(solution)/shard_map/transpose | solution.py:219
  254.5 1.0 copy.132
  255.6 2.5 constant_dynamic-update-slice_fusion.7
  258.0 3.7 fusion.2
  261.8 2.9 fusion.1
  264.7 1.6 fusion.17
  267.0 1.0 copy-done.14
  269.1 3.3 reduce.65
  272.3 0.8 reshape.781
  273.2 3.6 all-to-all-start.2
  276.8 3.9 fusion.39
  281.1 1.7 copy.113
  282.8 1.2 all-to-all-done.2
  284.0 3.6 all-to-all-start.4
  287.7 10.6 %all-to-all-done.4 = f32[1,256,768]{2,0,1:T(1,128)S(1)} async-done(((f32[1,256,768]{2,0,1:T(1,128)}), f32[1,256,768]{2,0,1:T(1,128)S(1)}, u32[]{:S(2)}, u32[]{:S(2)}) %all-to-all-start.4) | async-done | bytes 786464 | tf_op jit(solution)/shard_map/all_to_all | solution.py:190
  298.2 1.1 broadcast_in_dim.11
  299.4 2.6 all-to-all-start.5
  302.8 0.8 copy.126
  303.6 0.9 copy.127
  304.5 18.4 %all-to-all-done.5 = f32[32,1,4608]{2,1,0:T(1,128)S(1)} async-done(((f32[32,1,4608]{2,1,0:T(1,128)}), f32[32,1,4608]{2,1,0:T(1,128)S(1)}, u32[]{:S(2)}, u32[]{:S(2)}) %all-to-all-start.5) | async-done | bytes 589856 | tf_op jit(solution)/shard_map/all_to_all | solution.py:202
  323.9 3.5 all-to-all-start.6
  327.8 1.3 fusion.46
  329.7 6.0 %all-to-all-done.6 = f32[16,1,96]{2,1,0:T(1,128)S(1)} async-done(((f32[16,1,96]{2,1,0:T(1,128)}), f32[16,1,96]{2,1,0:T(1,128)S(1)}, u32[]{:S(2)}, u32[]{:S(2)}) %all-to-all-start.6) | async-done | bytes 6176 | tf_op jit(solution)/shard_map/all_to_all | solution.py:256
  337.6 92.9 %reduce-scatter.4.cloned.1.call-done = bf16[24,9344]{1,0:T(8,128)(2,1)} async-done(((bf16[768,9344]{1,0:T(8,128)(2,1)}), bf16[24,9344]{1,0:T(8,128)(2,1)}) %reduce-scatter.4.cloned.1.call-update) | async-done | bytes 448528
  430.5 1.1 convert_element_type.313
  432.8 1.7 fusion.84
  434.7 0.8 copy.119
  436.1 0.7 slice.130
  (128 shorter events, 16.4 us)
Async XLA Ops:
  7.2 35.3 %copy-start = (bf16[48,4608]{1,0:T(8,128)(2,1)S(1)}, bf16[48,4608]{1,0:T(8,128)(2,1)}, u32[]{:S(2)}) copy-start(bf16[48,4608]{1,0:T(8,128)(2,1)} %param.17) | copy-start | bytes 1327108
  7.2 67.3 %all-gather.5.cloned.1.call-start = ((), (), s32[]{:S(2)}) async-start(), calls=%async_computation.8 | async-start | bytes 3760128 | tf_op jit(solution)/shard_map/all_gather | solution.py:106
  7.9 96.6 %all-gather.7.cloned.1.call-start = ((), (), s32[]{:S(2)}) async-start(), calls=%async_computation.9 | async-start | bytes 1253376 | tf_op jit(solution)/shard_map/all_gather | solution.py:107
  8.7 150.2 %all-gather.11.cloned.1.call-start = ((), (), s32[]{:S(2)}) async-start(), calls=%async_computation.11 | async-start | bytes 5013504 | tf_op jit(solution)/shard_map/all_gather | solution.py:109
  9.4 203.3 %all-gather.9.cloned.1.call-start = ((), (), s32[]{:S(2)}) async-start(), calls=%async_computation.10 | async-start | bytes 5013504 | tf_op jit(solution)/shard_map/all_gather | solution.py:108
  10.0 33.7 %all-to-all-start = ((bf16[2,128,768]{2,1,0:T(8,128)(2,1)}), bf16[2,128,768]{2,1,0:T(8,128)(2,1)S(1)}, u32[]{:S(2)}, u32[]{:S(2)}) async-start(bf16[2,128,768]{2,1,0:T(8,128)(2,1)} %param.14), calls=%async_computation | async-start | bytes 786432 | tf_op jit(solution)/shard_map/all_to_all | solution.py:85
  43.7 18.0 %all-to-all-start.1 = ((f32[16,1,4608]{2,1,0:T(1,128)}), f32[16,1,4608]{2,1,0:T(1,128)S(1)}, u32[]{:S(2)}, u32[]{:S(2)}) async-start(f32[16,1,4608]{2,1,0:T(1,128)} %copy.104), calls=%async_computation.1 | async-start | bytes 589824 | tf_op jit(solution)/shard_map/all_to_all | solution.py:95
  61.7 10.5 %all-to-all-start.3 = ((bf16[2,128,768]{2,1,0:T(8,128)(2,1)}), bf16[2,128,768]{2,1,0:T(8,128)(2,1)S(1)}, u32[]{:S(2)}, u32[]{:S(2)}) async-start(bf16[2,128,768]{2,1,0:T(8,128)(2,1)} %param.16), calls=%async_computation.3 | async-start | bytes 786432 | tf_op jit(solution)/shard_map/all_to_all | solution.py:86
  65.5 365.0 %reduce-scatter.4.cloned.1.call-start = ((), (), s32[]{:S(2)}) async-start(), calls=%async_computation.12 | async-start | bytes 14800896
  212.7 7.0 %copy-start.16 = (bf16[768,3072]{1,0:T(8,128)(2,1)S(1)}, bf16[768,3072]{1,0:T(8,128)(2,1)}, u32[]{:S(2)}) copy-start(bf16[768,3072]{1,0:T(8,128)(2,1)} %all-gather.9.cloned.1.call-done) | copy-start | bytes 14155780
  219.7 1.5 copy-start.17
  219.8 2.4 copy-start.19
  219.8 4.0 copy-start.2
  226.7 2.0 copy-start.3
  228.0 0.8 copy-start.5
  230.2 5.0 %copy-start.12 = (bf16[256,768]{0,1:T(8,128)(2,1)S(1)}, bf16[256,768]{0,1:T(8,128)(2,1)}, u32[]{:S(2)}) copy-start(bf16[256,768]{0,1:T(8,128)(2,1)} %copy.109) | copy-start | bytes 1179652
  235.2 1.9 copy-start.1
  240.5 2.5 copy-start.9
  240.6 2.5 copy-start.20
  243.1 4.6 %copy-start.10 = (bf16[1,1,12,256,64]{3,4,2,1,0:T(8,128)(2,1)S(1)}, bf16[1,1,12,256,64]{3,4,2,1,0:T(8,128)(2,1)}, u32[]{:S(2)}) copy-start(bf16[1,1,12,256,64]{3,4,2,1,0:T(8,128)(2,1)} %fusion.22) | copy-start | bytes 1179652
  255.6 2.5 copy-start.18
  258.0 3.7 copy-start.13
  261.8 2.9 copy-start.6
  261.8 2.9 copy-start.11
  267.0 1.0 copy-start.14
  273.2 10.8 %all-to-all-start.2 = ((bf16[2,2,49152]{2,1,0:T(2,128)(2,1)}), bf16[2,2,49152]{2,1,0:T(2,128)(2,1)S(1)}, u32[]{:S(2)}, u32[]{:S(2)}) async-start(bf16[2,2,49152]{2,1,0:T(2,128)(2,1)} %reshape.781), calls=%async_computation.2 | async-start | bytes 786432 | tf_op jit(solution)/shard_map/all_to_all | solution.py:142
  276.8 4.0 copy-start.7
  276.8 4.0 copy-start.8
  284.0 14.2 %all-to-all-start.4 = ((f32[1,256,768]{2,0,1:T(1,128)}), f32[1,256,768]{2,0,1:T(1,128)S(1)}, u32[]{:S(2)}, u32[]{:S(2)}) async-start(f32[1,256,768]{2,0,1:T(1,128)} %copy.113), calls=%async_computation.4 | async-start | bytes 1572864 | tf_op jit(solution)/shard_map/all_to_all | solution.py:190
  299.4 23.6 %all-to-all-start.5 = ((f32[32,1,4608]{2,1,0:T(1,128)}), f32[32,1,4608]{2,1,0:T(1,128)S(1)}, u32[]{:S(2)}, u32[]{:S(2)}) async-start(f32[32,1,4608]{2,1,0:T(1,128)} %broadcast_in_dim.11), calls=%async_computation.5 | async-start | bytes 1179648 | tf_op jit(solution)/shard_map/all_to_all | solution.py:202
  302.4 34.6 %copy-start.15 = (bf16[2,768]{1,0:T(2,128)(2,1)S(1)}, bf16[2,768]{1,0:T(2,128)(2,1)}, u32[]{:S(2)}) copy-start(bf16[2,768]{1,0:T(2,128)(2,1)} %param.15) | copy-start | bytes 9220
  323.9 11.8 %all-to-all-start.6 = ((f32[16,1,96]{2,1,0:T(1,128)}), f32[16,1,96]{2,1,0:T(1,128)S(1)}, u32[]{:S(2)}, u32[]{:S(2)}) async-start(f32[16,1,96]{2,1,0:T(1,128)} %bitcast.29), calls=%async_computation.6 | async-start | bytes 16384 | tf_op jit(solution)/shard_map/all_to_all | solution.py:256
  430.5 5.0 %copy-start.4 = (bf16[24,9344]{1,0:T(8,128)(2,1)S(1)}, bf16[24,9344]{1,0:T(8,128)(2,1)}, u32[]{:S(2)}) copy-start(bf16[24,9344]{1,0:T(8,128)(2,1)} %reduce-scatter.4.cloned.1.call-done) | copy-start | bytes 1345540
Sparse Core Ops, SparseCore 0:
  10.3 55.0 all-gather.4
  67.7 36.8 all-gather.6
  106.9 51.9 all-gather.10
  161.0 51.6 all-gather.8
  267.1 163.3 reduce-scatter.3
where the time goes:
time: 444 us; the launch traced here: 443 us
  waiting for transfers between devices  268 us (60%)
  matrix products  58 us (13%)
  local copies, waits for them, and re-layouts  38.8 us (9%)
  starting transfers between devices  24.9 us (6%)
  blocking collectives  22.7 us (5%)
  other arithmetic  16.2 us (4%)
  between operations  14.4 us (3%)
    unnamed x6, waiting for transfers between devices  95.5 us
    all_gather x1, waiting for transfers between devices, body(): down_full = lax.all_gather(w_down, 'fsdp', axis=0, tiled=True)  51.3 us
    all_gather x1, waiting for transfers between devices, body(): up_full = lax.all_gather(w_up, 'fsdp', axis=0, tiled=True)  48.2 us
    all_gather x1, blocking collectives, body(): lax.all_gather(jnp.concatenate(small).reshape(1, padded // 128, 128), 'fs...  22.7 us
    all_to_all x1, waiting for transfers between devices, body(): lax.all_to_all(jnp.broadcast_to(grad_mod[None], (owners, own_latents, 6 *...  18.4 us
    all_gather x1, waiting for transfers between devices, body(): out_full = lax.all_gather(w_out, 'fsdp', axis=0, tiled=True)  17.1 us
    all_to_all x1, waiting for transfers between devices, body(): lax.all_to_all(mod_part.reshape(fsdp_count, own_latents * 6 * D), 'fsdp',...  13.7 us
    unnamed x55, local copies, waits for them, and re-layouts  12.7 us
  transfers between devices with their start and end apart: 12, of which 10 were waited for; matrix products, arithmetic and copies ran while one was open for 12% of the time, Pallas kernels for 0%

commit v1 on v0

--- a/solution.py
+++ b/solution.py
@@ -106,7 +106,17 @@
     qkv_full = lax.all_gather(w_qkv, "fsdp", axis=0, tiled=True)
     out_full = lax.all_gather(w_out, "fsdp", axis=0, tiled=True)
     up_full = lax.all_gather(w_up, "fsdp", axis=0, tiled=True)
-    down_full = lax.all_gather(w_down, "fsdp", axis=0, tiled=True)
+    patch = w_down
+    w1, out_arr, block_now = (lax.axis_size("fsdp"), lax.axis_index("fsdp"), patch.shape[0])
+    windows = [kk * w1 if j == 0 else kk for j, kk in enumerate(patch.shape)]
+    down_full = lax.dynamic_update_slice_in_dim(
+        jnp.zeros(windows, patch.dtype), patch, out_arr * block_now, axis=0
+    )
+    for k0 in range(1, w1):
+        patch = lax.ppermute(patch, "fsdp", [(j, (j + 1) % w1) for j in range(w1)])
+        down_full = lax.dynamic_update_slice_in_dim(
+            down_full, patch, (out_arr - k0) % w1 * block_now, axis=0
+        )
     normed_one, inverse_one = normalize(inputs)
     attn_in = (normed_one * (1.0 + scale_one) + shift_one).astype(bf16)
     qkv_bias = jnp.concatenate([query_bias, jnp.zeros_like(query_bias), value_bias]).astype(f32)

time: 444 us -> 444 us (level); the launches traced: 443 us -> 438 us
  waiting for transfers between devices: 268 us -> 250 us
  local copies, waits for them, and re-layouts: 38.8 us -> 53.4 us
    ppermute x0 -> x15, waiting for transfers between devices: none -> 122 us  [body(): patch = lax.ppermute(patch, 'fsdp', [(j, (j + 1) % w1) for j in range(w1)])]
    all_gather x1 -> x0, waiting for transfers between devices: 51.3 us -> none  [body(): down_full = lax.all_gather(w_down, 'fsdp', axis=0, tiled=True)]
    all_gather x1, waiting for transfers between devices: 48.2 us -> 0.02 us  [body(): up_full = lax.all_gather(w_up, 'fsdp', axis=0, tiled=True)]
    all_gather x1, waiting for transfers between devices: 17.1 us -> 0.01 us  [body(): out_full = lax.all_gather(w_out, 'fsdp', axis=0, tiled=True)]
    dynamic_update_slice x0 -> x16, local copies, waits for them, and re-layouts: none -> 15.7 us  [the longest x15 15 us: body(): lax.dynamic_update_slice_in_dim(down_full, patch, (out_arr - k0) % w1 * b...]
    all_to_all x1, waiting for transfers between devices: 13.7 us -> 0.01 us  [body(): lax.all_to_all(mod_part.reshape(fsdp_count, own_latents * 6 * D), 'fsdp',...]
    all_to_all x1, waiting for transfers between devices: 6.41 us -> 0.01 us  [body(): lax.all_to_all(cotangent, 'sp', split_axis=0, concat_axis=1, tiled=True)]
    unnamed x55 -> x59, local copies, waits for them, and re-layouts: 12.7 us -> 11 us
  transfers between devices with their start and end apart: 12 -> 26, of which waited for: 10 -> 18; matrix products, arithmetic and copies ran while one was open for 12% -> 15% of each run, Pallas kernels for 0% -> 0%
where the time goes in v1:
time: 444 us; the launch traced here: 438 us
  waiting for transfers between devices  250 us (56%)
  matrix products  54.1 us (12%)
  local copies, waits for them, and re-layouts  53.4 us (12%)
  starting transfers between devices  27.8 us (6%)
  blocking collectives  22.8 us (5%)
  between operations  15.1 us (3%)
  other arithmetic  14.9 us (3%)
    ppermute x15, waiting for transfers between devices, body(): patch = lax.ppermute(patch, 'fsdp', [(j, (j + 1) % w1) for j in range(w1)])  122 us
    unnamed x5, waiting for transfers between devices  94.9 us
    all_gather x1, blocking collectives, body(): lax.all_gather(jnp.concatenate(small).reshape(1, padded // 128, 128), 'fs...  22.8 us
    all_to_all x1, waiting for transfers between devices, body(): lax.all_to_all(jnp.broadcast_to(grad_mod[None], (owners, own_latents, 6 *...  18.5 us
    dynamic_update_slice x15, local copies, waits for them, and re-layouts, body(): lax.dynamic_update_slice_in_dim(down_full, patch, (out_arr - k0) % w1 * b...  15 us
    unnamed x59, local copies, waits for them, and re-layouts  11 us
  transfers between devices with their start and end apart: 26, of which 18 were waited for; matrix products, arithmetic and copies ran while one was open for 15% of the time, Pallas kernels for 0%

profile of v1, /device:TPU:0, one launch (start us, length us, event | category | flops | bytes accessed | tf_op | source)
XLA Modules:
  0.0 437.9 jit_solution(11525001162575732519)
XLA Ops:
  10.0 3.8 all-to-all-start
  14.4 4.1 concatenate.24
  18.5 22.8 %all_gather.12 = bf16[16,32,128]{2,1,0:T(8,128)(2,1)S(1)} all-gather(bf16[1,32,128]{2,1,0:T(8,128)(2,1)S(1)} %bitcast.188), channel_id=1, replica_groups=mesh['fsdp'=16,'sp'=2] {'fsdp'}, dimensions={0}, use_global_device_ids=true | all-gather | bytes 139264 | tf_op jit(solution)/shard_map/all_gather | solution.py:74
  42.0 14.3 %collective-permute-done.1 = bf16[192,768]{1,0:T(8,128)(2,1)S(1)} collective-permute-done((bf16[192,768]{1,0:T(8,128)(2,1)S(1)}, bf16[192,768]{1,0:T(8,128)(2,1)S(1)}, u32[]{:S(2)}, u32[]{:S(2)}) %collective-permute-start.1) | collective-permute-done | bytes 294944 | tf_op jit(solution)/shard_map/ppermute | solution.py:116
  56.7 10.0 %collective-permute-done.2 = bf16[192,768]{1,0:T(8,128)(2,1)S(1)} collective-permute-done((bf16[192,768]{1,0:T(8,128)(2,1)S(1)}, bf16[192,768]{1,0:T(8,128)(2,1)S(1)}, u32[]{:S(2)}, u32[]{:S(2)}) %collective-permute-start.2) | collective-permute-done | bytes 294944 | tf_op jit(solution)/shard_map/ppermute | solution.py:116
  66.7 8.7 %collective-permute-done.3 = bf16[192,768]{1,0:T(8,128)(2,1)S(1)} collective-permute-done((bf16[192,768]{1,0:T(8,128)(2,1)S(1)}, bf16[192,768]{1,0:T(8,128)(2,1)S(1)}, u32[]{:S(2)}, u32[]{:S(2)}) %collective-permute-start.3) | collective-permute-done | bytes 294944 | tf_op jit(solution)/shard_map/ppermute | solution.py:116
  75.7 9.9 %collective-permute-done.4 = bf16[192,768]{1,0:T(8,128)(2,1)S(1)} collective-permute-done((bf16[192,768]{1,0:T(8,128)(2,1)S(1)}, bf16[192,768]{1,0:T(8,128)(2,1)S(1)}, u32[]{:S(2)}, u32[]{:S(2)}) %collective-permute-start.4) | collective-permute-done | bytes 294944 | tf_op jit(solution)/shard_map/ppermute | solution.py:116
  85.9 1.0 copy.104
  87.3 2.5 broadcast_in_dim.12
  90.5 5.9 %all-to-all-start.1 = ((f32[16,1,4608]{2,1,0:T(1,128)}), f32[16,1,4608]{2,1,0:T(1,128)S(1)}, u32[]{:S(2)}, u32[]{:S(2)}) async-start(f32[16,1,4608]{2,1,0:T(1,128)} %copy.104), calls=%async_computation.1 | async-start | bytes 589824 | tf_op jit(solution)/shard_map/all_to_all | solution.py:95
  97.2 14.1 %collective-permute-done.6 = bf16[192,768]{1,0:T(8,128)(2,1)} collective-permute-done((bf16[192,768]{1,0:T(8,128)(2,1)}, bf16[192,768]{1,0:T(8,128)(2,1)}, u32[]{:S(2)}, u32[]{:S(2)}) %collective-permute-start.6) | collective-permute-done | bytes 294944 | tf_op jit(solution)/shard_map/ppermute | solution.py:116
  112.1 3.5 all-to-all-start.3
  115.9 4.7 %collective-permute-done.7 = bf16[192,768]{1,0:T(8,128)(2,1)} collective-permute-done((bf16[192,768]{1,0:T(8,128)(2,1)}, bf16[192,768]{1,0:T(8,128)(2,1)}, u32[]{:S(2)}, u32[]{:S(2)}) %collective-permute-start.7) | collective-permute-done | bytes 294944 | tf_op jit(solution)/shard_map/ppermute | solution.py:116
  120.9 14.5 %collective-permute-done.8 = bf16[192,768]{1,0:T(8,128)(2,1)S(1)} collective-permute-done((bf16[192,768]{1,0:T(8,128)(2,1)}, bf16[192,768]{1,0:T(8,128)(2,1)S(1)}, u32[]{:S(2)}, u32[]{:S(2)}) %collective-permute-start.8) | collective-permute-done | bytes 294944 | tf_op jit(solution)/shard_map/ppermute | solution.py:116
  135.6 1.0 fusion.43
  136.6 9.5 %collective-permute-done.9 = bf16[192,768]{1,0:T(8,128)(2,1)} collective-permute-done((bf16[192,768]{1,0:T(8,128)(2,1)S(1)}, bf16[192,768]{1,0:T(8,128)(2,1)}, u32[]{:S(2)}, u32[]{:S(2)}) %collective-permute-start.9) | collective-permute-done | bytes 294944 | tf_op jit(solution)/shard_map/ppermute | solution.py:116
  147.7 12.4 %collective-permute-done.10 = bf16[192,768]{1,0:T(8,128)(2,1)S(1)} collective-permute-done((bf16[192,768]{1,0:T(8,128)(2,1)}, bf16[192,768]{1,0:T(8,128)(2,1)S(1)}, u32[]{:S(2)}, u32[]{:S(2)}) %collective-permute-start.10) | collective-permute-done | bytes 294944 | tf_op jit(solution)/shard_map/ppermute | solution.py:116
  162.4 7.4 %collective-permute-done.11 = bf16[192,768]{1,0:T(8,128)(2,1)S(1)} collective-permute-done((bf16[192,768]{1,0:T(8,128)(2,1)S(1)}, bf16[192,768]{1,0:T(8,128)(2,1)S(1)}, u32[]{:S(2)}, u32[]{:S(2)}) %collective-permute-start.11) | collective-permute-done | bytes 294944 | tf_op jit(solution)/shard_map/ppermute | solution.py:116
  169.8 1.7 constant_dynamic-update-slice_fusion.17
  171.5 1.7 constant_dynamic-update-slice_fusion.16
  173.2 1.7 constant_dynamic-update-slice_fusion.15
  174.9 3.8 collective-permute-done.12
  179.4 1.7 constant_dynamic-update-slice_fusion.13
  181.8 5.7 %collective-permute-done.13 = bf16[192,768]{1,0:T(8,128)(2,1)S(1)} collective-permute-done((bf16[192,768]{1,0:T(8,128)(2,1)S(1)}, bf16[192,768]{1,0:T(8,128)(2,1)S(1)}, u32[]{:S(2)}, u32[]{:S(2)}) %collective-permute-start.13) | collective-permute-done | bytes 294944 | tf_op jit(solution)/shard_map/ppermute | solution.py:116
  189.7 6.7 %collective-permute-done.14 = bf16[192,768]{1,0:T(8,128)(2,1)S(1)} collective-permute-done((bf16[192,768]{1,0:T(8,128)(2,1)S(1)}, bf16[192,768]{1,0:T(8,128)(2,1)S(1)}, u32[]{:S(2)}, u32[]{:S(2)}) %collective-permute-start.14) | collective-permute-done | bytes 294944 | tf_op jit(solution)/shard_map/ppermute | solution.py:116
  197.1 4.1 fusion.3
  201.2 2.0 copy.105
  203.2 2.2 fusion.60
  205.5 4.8 %convolution_convert_fusion.4 = bf16[12,256,64]{1,2,0:T(8,128)(2,1)} fusion(f32[12,256,256]{1,2,0:T(8,128)} %fusion.60, bf16[3,1,12,256,64]{3,4,2,1,0:T(8,128)(2,1)S(1)} %bitcast.160), kind=kOutput, calls=%fused_computation.34 | convolution fusion | flops 104008960 | bytes 7077888 | tf_op jit(solution)/shard_map/bhqk,bhkd->bhqd/dot_general | solution.py:134
  210.2 2.8 fusion.83
  213.3 4.0 convolution_add_fusion.1
  217.3 6.4 %fusion.80 = (bf16[3072]{0:T(1024)(128)(2,1)S(1)}, bf16[256,3072]{1,0:T(8,128)(2,1)S(1)}) fusion(f32[256,3072]{1,0:T(8,128)S(1)} %convolution_add_fusion.1, bf16[256,768]{1,0:T(8,128)(2,1)S(1)} %copy-done.12, bf16[3072,768]{1,0:T(8,128)(2,1)} %constant_dynamic-update-slice_fusion.8), kind=kOutput, calls=%fused_computation.169 | convolution fusion | flops 1224471552 | bytes 9836544 | tf_op jit(solution)/shard_map/btd,fd->btf/dot_general | solution.py:157
  223.7 1.4 fusion.86
  225.2 5.2 %fusion.25 = (f32[768]{0:T(1024)S(1)}, bf16[1,256,768]{2,1,0:T(8,128)(2,1)}, f32[768]{0:T(1024)S(1)}, f32[256]{0:T(256)S(1)}, f32[256]{0:T(256)S(1)}, /*index=5*/f32[768]{0:T(1024)S(1)}) fusion(bf16[2,128,768]{2,1,0:T(8,128)(2,1)S(1)} %all-to-all-done.3, f32[256,768]{1,0:T(8,128)S(1)} %get-tuple-element.36, f32[768]{0:T(1024)S(1)} %get-tuple-element.24, ...), kind=kOutput, calls=%fused_computation.51 | convolution fusion | flops 1218180352 | bytes 10246144 | tf_op jit(solution)/shard_map/btf,fd->btd/dot_general | solution.py:148
  230.4 1.3 fusion.82
  233.0 0.9 copy.109
  233.9 4.8 %fusion.20 = bf16[1,1,12,256,64]{3,4,2,1,0:T(8,128)(2,1)} fusion(bf16[12,256,64]{1,2,0:T(8,128)(2,1)} %bitcast.174, f32[12,256,256]{1,2,0:T(8,128)} %fusion.60), kind=kOutput, calls=%fused_computation.39 | convolution fusion | flops 104008960 | bytes 3932160 | tf_op jit(solution)/shard_map/bhqk,bhqd->bhkd/dot_general | solution.py:184
  239.5 1.1 copy-done.1
  240.6 2.6 multiply_reduce_fusion
  244.9 1.0 copy-done.20
  245.9 2.3 convolution_convert_fusion.2
  248.2 2.3 copy.117
  250.5 1.0 copy.132
  251.6 2.5 constant_dynamic-update-slice_fusion.7
  254.1 3.8 fusion.2
  258.0 3.0 fusion.1
  261.0 1.5 fusion.17
  264.3 1.0 copy-done.14
  266.4 3.2 reduce.65
  270.5 3.5 all-to-all-start.2
  274.0 3.9 fusion.39
  278.4 1.7 copy.113
  281.0 3.6 all-to-all-start.4
  284.7 7.9 %all-to-all-done.4 = f32[1,256,768]{2,0,1:T(1,128)S(1)} async-done(((f32[1,256,768]{2,0,1:T(1,128)}), f32[1,256,768]{2,0,1:T(1,128)S(1)}, u32[]{:S(2)}, u32[]{:S(2)}) %all-to-all-start.4) | async-done | bytes 786464 | tf_op jit(solution)/shard_map/all_to_all | solution.py:200
  292.5 1.1 broadcast_in_dim.14
  293.7 2.6 all-to-all-start.5
  297.9 0.9 copy.127
  298.9 18.5 %all-to-all-done.5 = f32[32,1,4608]{2,1,0:T(1,128)S(1)} async-done(((f32[32,1,4608]{2,1,0:T(1,128)}), f32[32,1,4608]{2,1,0:T(1,128)S(1)}, u32[]{:S(2)}, u32[]{:S(2)}) %all-to-all-start.5) | async-done | bytes 589856 | tf_op jit(solution)/shard_map/all_to_all | solution.py:212
  318.2 3.5 all-to-all-start.6
  322.2 1.3 fusion.46
  324.1 5.9 %all-to-all-done.6 = f32[16,1,96]{2,1,0:T(1,128)S(1)} async-done(((f32[16,1,96]{2,1,0:T(1,128)}), f32[16,1,96]{2,1,0:T(1,128)S(1)}, u32[]{:S(2)}, u32[]{:S(2)}) %all-to-all-start.6) | async-done | bytes 6176 | tf_op jit(solution)/shard_map/all_to_all | solution.py:266
  332.0 92.8 %reduce-scatter.4.cloned.1.call-done = bf16[24,9344]{1,0:T(8,128)(2,1)} async-done(((bf16[768,9344]{1,0:T(8,128)(2,1)}), bf16[24,9344]{1,0:T(8,128)(2,1)}) %reduce-scatter.4.cloned.1.call-update) | async-done | bytes 448528
  424.8 1.1 convert_element_type.313
  427.1 1.7 fusion.84
  (177 shorter events, 34.5 us)
Async XLA Ops:
  7.2 68.3 %copy-start = (bf16[48,4608]{1,0:T(8,128)(2,1)S(1)}, bf16[48,4608]{1,0:T(8,128)(2,1)}, u32[]{:S(2)}) copy-start(bf16[48,4608]{1,0:T(8,128)(2,1)} %param.17) | copy-start | bytes 1327108
  7.2 189.9 %all-gather.4.cloned.1.call-start = ((), (), s32[]{:S(2)}) async-start(), calls=%async_computation.8 | async-start | bytes 3760128 | tf_op jit(solution)/shard_map/all_gather | solution.py:106
  7.9 202.3 %all-gather.6.cloned.1.call-start = ((), (), s32[]{:S(2)}) async-start(), calls=%async_computation.9 | async-start | bytes 1253376 | tf_op jit(solution)/shard_map/all_gather | solution.py:107
  8.7 204.6 %all-gather.8.cloned.1.call-start = ((), (), s32[]{:S(2)}) async-start(), calls=%async_computation.10 | async-start | bytes 5013504 | tf_op jit(solution)/shard_map/all_gather | solution.py:108
  9.4 32.0 %collective-permute-start = (bf16[192,768]{1,0:T(8,128)(2,1)}, bf16[192,768]{1,0:T(8,128)(2,1)S(1)}, u32[]{:S(2)}, u32[]{:S(2)}) collective-permute-start(bf16[192,768]{1,0:T(8,128)(2,1)} %param.26), channel_id=1, source_target_pairs={{0,2},{2,4},{4,6},{6,8},{8,10},{10,12},{12,14},{14,16},{16,18},{18... | collective-permute-start | bytes 884744 | tf_op jit(solution)/shard_map/ppermute | solution.py:116
  10.0 80.5 %all-to-all-start = ((bf16[2,128,768]{2,1,0:T(8,128)(2,1)}), bf16[2,128,768]{2,1,0:T(8,128)(2,1)S(1)}, u32[]{:S(2)}, u32[]{:S(2)}) async-start(bf16[2,128,768]{2,1,0:T(8,128)(2,1)} %param.14), calls=%async_computation | async-start | bytes 786432 | tf_op jit(solution)/shard_map/all_to_all | solution.py:85
  41.4 14.8 %collective-permute-start.1 = (bf16[192,768]{1,0:T(8,128)(2,1)S(1)}, bf16[192,768]{1,0:T(8,128)(2,1)S(1)}, u32[]{:S(2)}, u32[]{:S(2)}) collective-permute-start(bf16[192,768]{1,0:T(8,128)(2,1)S(1)} %collective-permute-done), channel_id=1, source_target_pairs={{0,2},{2,4},{4,6},{6,8},{8,10},{10,12},{12,14},{14,16},{16,18},{18... | collective-permute-start | bytes 884744 | tf_op jit(solution)/shard_map/ppermute | solution.py:116
  56.3 10.4 %collective-permute-start.2 = (bf16[192,768]{1,0:T(8,128)(2,1)S(1)}, bf16[192,768]{1,0:T(8,128)(2,1)S(1)}, u32[]{:S(2)}, u32[]{:S(2)}) collective-permute-start(bf16[192,768]{1,0:T(8,128)(2,1)S(1)} %collective-permute-done.1), channel_id=1, source_target_pairs={{0,2},{2,4},{4,6},{6,8},{8,10},{10,12},{12,14},{14,16},{16,18},{18... | collective-permute-start | bytes 884744 | tf_op jit(solution)/shard_map/ppermute | solution.py:116
  66.6 8.8 %collective-permute-start.3 = (bf16[192,768]{1,0:T(8,128)(2,1)S(1)}, bf16[192,768]{1,0:T(8,128)(2,1)S(1)}, u32[]{:S(2)}, u32[]{:S(2)}) collective-permute-start(bf16[192,768]{1,0:T(8,128)(2,1)S(1)} %collective-permute-done.2), channel_id=1, source_target_pairs={{0,2},{2,4},{4,6},{6,8},{8,10},{10,12},{12,14},{14,16},{16,18},{18... | collective-permute-start | bytes 884744 | tf_op jit(solution)/shard_map/ppermute | solution.py:116
  75.5 10.1 %collective-permute-start.4 = (bf16[192,768]{1,0:T(8,128)(2,1)S(1)}, bf16[192,768]{1,0:T(8,128)(2,1)S(1)}, u32[]{:S(2)}, u32[]{:S(2)}) collective-permute-start(bf16[192,768]{1,0:T(8,128)(2,1)S(1)} %collective-permute-done.3), channel_id=1, source_target_pairs={{0,2},{2,4},{4,6},{6,8},{8,10},{10,12},{12,14},{14,16},{16,18},{18... | collective-permute-start | bytes 884744 | tf_op jit(solution)/shard_map/ppermute | solution.py:116
  75.7 14.1 %copy-start.15 = (bf16[192,768]{1,0:T(8,128)(2,1)S(1)}, bf16[192,768]{1,0:T(8,128)(2,1)}, u32[]{:S(2)}) copy-start(bf16[192,768]{1,0:T(8,128)(2,1)} %param.26) | copy-start | bytes 884740
  85.6 10.9 %collective-permute-start.5 = (bf16[192,768]{1,0:T(8,128)(2,1)S(1)}, bf16[192,768]{1,0:T(8,128)(2,1)}, u32[]{:S(2)}, u32[]{:S(2)}) collective-permute-start(bf16[192,768]{1,0:T(8,128)(2,1)S(1)} %collective-permute-done.4), channel_id=1, source_target_pairs={{0,2},{2,4},{4,6},{6,8},{8,10},{10,12},{12,14},{14,16},{16,18},{18... | collective-permute-start | bytes 884744 | tf_op jit(solution)/shard_map/ppermute | solution.py:116
  90.5 21.7 %all-to-all-start.1 = ((f32[16,1,4608]{2,1,0:T(1,128)}), f32[16,1,4608]{2,1,0:T(1,128)S(1)}, u32[]{:S(2)}, u32[]{:S(2)}) async-start(f32[16,1,4608]{2,1,0:T(1,128)} %copy.104), calls=%async_computation.1 | async-start | bytes 589824 | tf_op jit(solution)/shard_map/all_to_all | solution.py:95
  96.5 14.9 %collective-permute-start.6 = (bf16[192,768]{1,0:T(8,128)(2,1)}, bf16[192,768]{1,0:T(8,128)(2,1)}, u32[]{:S(2)}, u32[]{:S(2)}) collective-permute-start(bf16[192,768]{1,0:T(8,128)(2,1)} %collective-permute-done.5), channel_id=1, source_target_pairs={{0,2},{2,4},{4,6},{6,8},{8,10},{10,12},{12,14},{14,16},{16,18},{18... | collective-permute-start | bytes 884744 | tf_op jit(solution)/shard_map/ppermute | solution.py:116
  111.3 9.2 %collective-permute-start.7 = (bf16[192,768]{1,0:T(8,128)(2,1)}, bf16[192,768]{1,0:T(8,128)(2,1)}, u32[]{:S(2)}, u32[]{:S(2)}) collective-permute-start(bf16[192,768]{1,0:T(8,128)(2,1)} %collective-permute-done.6), channel_id=1, source_target_pairs={{0,2},{2,4},{4,6},{6,8},{8,10},{10,12},{12,14},{14,16},{16,18},{18... | collective-permute-start | bytes 884744 | tf_op jit(solution)/shard_map/ppermute | solution.py:116
  112.1 23.3 %all-to-all-start.3 = ((bf16[2,128,768]{2,1,0:T(8,128)(2,1)}), bf16[2,128,768]{2,1,0:T(8,128)(2,1)S(1)}, u32[]{:S(2)}, u32[]{:S(2)}) async-start(bf16[2,128,768]{2,1,0:T(8,128)(2,1)} %param.16), calls=%async_computation.3 | async-start | bytes 786432 | tf_op jit(solution)/shard_map/all_to_all | solution.py:86
  115.6 309.2 %reduce-scatter.4.cloned.1.call-start = ((), (), s32[]{:S(2)}) async-start(), calls=%async_computation.11 | async-start | bytes 14800896
  120.6 14.8 %collective-permute-start.8 = (bf16[192,768]{1,0:T(8,128)(2,1)}, bf16[192,768]{1,0:T(8,128)(2,1)S(1)}, u32[]{:S(2)}, u32[]{:S(2)}) collective-permute-start(bf16[192,768]{1,0:T(8,128)(2,1)} %collective-permute-done.7), channel_id=1, source_target_pairs={{0,2},{2,4},{4,6},{6,8},{8,10},{10,12},{12,14},{14,16},{16,18},{18... | collective-permute-start | bytes 884744 | tf_op jit(solution)/shard_map/ppermute | solution.py:116
  135.4 10.8 %collective-permute-start.9 = (bf16[192,768]{1,0:T(8,128)(2,1)S(1)}, bf16[192,768]{1,0:T(8,128)(2,1)}, u32[]{:S(2)}, u32[]{:S(2)}) collective-permute-start(bf16[192,768]{1,0:T(8,128)(2,1)S(1)} %collective-permute-done.8), channel_id=1, source_target_pairs={{0,2},{2,4},{4,6},{6,8},{8,10},{10,12},{12,14},{14,16},{16,18},{18... | collective-permute-start | bytes 884744 | tf_op jit(solution)/shard_map/ppermute | solution.py:116
  146.2 13.9 %collective-permute-start.10 = (bf16[192,768]{1,0:T(8,128)(2,1)}, bf16[192,768]{1,0:T(8,128)(2,1)S(1)}, u32[]{:S(2)}, u32[]{:S(2)}) collective-permute-start(bf16[192,768]{1,0:T(8,128)(2,1)} %collective-permute-done.9), channel_id=1, source_target_pairs={{0,2},{2,4},{4,6},{6,8},{8,10},{10,12},{12,14},{14,16},{16,18},{18... | collective-permute-start | bytes 884744 | tf_op jit(solution)/shard_map/ppermute | solution.py:116
  160.1 9.7 %collective-permute-start.11 = (bf16[192,768]{1,0:T(8,128)(2,1)S(1)}, bf16[192,768]{1,0:T(8,128)(2,1)S(1)}, u32[]{:S(2)}, u32[]{:S(2)}) collective-permute-start(bf16[192,768]{1,0:T(8,128)(2,1)S(1)} %collective-permute-done.10), channel_id=1, source_target_pairs={{0,2},{2,4},{4,6},{6,8},{8,10},{10,12},{12,14},{14,16},{16,18},{18... | collective-permute-start | bytes 884744 | tf_op jit(solution)/shard_map/ppermute | solution.py:116
  169.8 8.8 %collective-permute-start.12 = (bf16[192,768]{1,0:T(8,128)(2,1)S(1)}, bf16[192,768]{1,0:T(8,128)(2,1)S(1)}, u32[]{:S(2)}, u32[]{:S(2)}) collective-permute-start(bf16[192,768]{1,0:T(8,128)(2,1)S(1)} %collective-permute-done.11), channel_id=1, source_target_pairs={{0,2},{2,4},{4,6},{6,8},{8,10},{10,12},{12,14},{14,16},{16,18},{18... | collective-permute-start | bytes 884744 | tf_op jit(solution)/shard_map/ppermute | solution.py:116
  178.6 8.8 %collective-permute-start.13 = (bf16[192,768]{1,0:T(8,128)(2,1)S(1)}, bf16[192,768]{1,0:T(8,128)(2,1)S(1)}, u32[]{:S(2)}, u32[]{:S(2)}) collective-permute-start(bf16[192,768]{1,0:T(8,128)(2,1)S(1)} %collective-permute-done.12), channel_id=1, source_target_pairs={{0,2},{2,4},{4,6},{6,8},{8,10},{10,12},{12,14},{14,16},{16,18},{18... | collective-permute-start | bytes 884744 | tf_op jit(solution)/shard_map/ppermute | solution.py:116
  187.5 8.8 %collective-permute-start.14 = (bf16[192,768]{1,0:T(8,128)(2,1)S(1)}, bf16[192,768]{1,0:T(8,128)(2,1)S(1)}, u32[]{:S(2)}, u32[]{:S(2)}) collective-permute-start(bf16[192,768]{1,0:T(8,128)(2,1)S(1)} %collective-permute-done.13), channel_id=1, source_target_pairs={{0,2},{2,4},{4,6},{6,8},{8,10},{10,12},{12,14},{14,16},{16,18},{18... | collective-permute-start | bytes 884744 | tf_op jit(solution)/shard_map/ppermute | solution.py:116
  213.3 4.0 copy-start.12
  213.3 10.4 %slice-start = ((s8[4718592]{0:T(1024)(128)(4,1)}), s8[4194304]{0:T(1024)(128)(4,1)S(1)}, s32[]{:S(2)}) async-start(s8[4718592]{0:T(1024)(128)(4,1)} %bitcast.190), calls=%async_computation.12 | async-start | bytes 8388608
  217.3 7.9 %copy-start.19 = (f32[256,3072]{1,0:T(8,128)}, f32[256,3072]{1,0:T(8,128)S(1)}, u32[]{:S(2)}) copy-start(f32[256,3072]{1,0:T(8,128)S(1)} %convolution_add_fusion.1) | copy-start | bytes 9437188
  217.3 6.4 %slice-start.1 = ((s8[4718592]{0:T(1024)(128)(4,1)}), s8[524288]{0:T(1024)(128)(4,1)S(1)}, s32[]{:S(2)}) async-start(s8[4718592]{0:T(1024)(128)(4,1)} %bitcast.190), calls=%async_computation.13 | async-start | bytes 1048576
  223.7 1.5 copy-start.17
  230.4 2.0 copy-start.2
  231.7 0.7 copy-start.4
  233.9 4.8 %copy-start.9 = (bf16[256,768]{0,1:T(8,128)(2,1)S(1)}, bf16[256,768]{0,1:T(8,128)(2,1)}, u32[]{:S(2)}) copy-start(bf16[256,768]{0,1:T(8,128)(2,1)} %copy.109) | copy-start | bytes 1179652
  238.7 1.9 copy-start.1
  243.9 1.0 copy-start.13
  243.9 2.0 copy-start.20
  251.6 2.5 copy-start.18
  254.1 3.8 copy-start.10
  254.1 3.9 copy-start.11
  258.0 3.0 copy-start.5
  258.0 3.0 copy-start.8
  264.3 1.0 copy-start.14
  270.5 10.5 %all-to-all-start.2 = ((bf16[2,2,49152]{2,1,0:T(2,128)(2,1)}), bf16[2,2,49152]{2,1,0:T(2,128)(2,1)S(1)}, u32[]{:S(2)}, u32[]{:S(2)}) async-start(bf16[2,2,49152]{2,1,0:T(2,128)(2,1)} %reshape.781), calls=%async_computation.2 | async-start | bytes 786432 | tf_op jit(solution)/shard_map/all_to_all | solution.py:152
  274.0 3.9 copy-start.6
  274.0 3.9 copy-start.7
  281.0 11.6 %all-to-all-start.4 = ((f32[1,256,768]{2,0,1:T(1,128)}), f32[1,256,768]{2,0,1:T(1,128)S(1)}, u32[]{:S(2)}, u32[]{:S(2)}) async-start(f32[1,256,768]{2,0,1:T(1,128)} %copy.113), calls=%async_computation.4 | async-start | bytes 1572864 | tf_op jit(solution)/shard_map/all_to_all | solution.py:200
  293.7 23.7 %all-to-all-start.5 = ((f32[32,1,4608]{2,1,0:T(1,128)}), f32[32,1,4608]{2,1,0:T(1,128)S(1)}, u32[]{:S(2)}, u32[]{:S(2)}) async-start(f32[32,1,4608]{2,1,0:T(1,128)} %broadcast_in_dim.14), calls=%async_computation.5 | async-start | bytes 1179648 | tf_op jit(solution)/shard_map/all_to_all | solution.py:212
  296.7 34.7 %copy-start.16 = (bf16[2,768]{1,0:T(2,128)(2,1)S(1)}, bf16[2,768]{1,0:T(2,128)(2,1)}, u32[]{:S(2)}) copy-start(bf16[2,768]{1,0:T(2,128)(2,1)} %param.15) | copy-start | bytes 9220
  318.2 11.8 %all-to-all-start.6 = ((f32[16,1,96]{2,1,0:T(1,128)}), f32[16,1,96]{2,1,0:T(1,128)S(1)}, u32[]{:S(2)}, u32[]{:S(2)}) async-start(f32[16,1,96]{2,1,0:T(1,128)} %bitcast.29), calls=%async_computation.6 | async-start | bytes 16384 | tf_op jit(solution)/shard_map/all_to_all | solution.py:266
  424.8 5.0 %copy-start.3 = (bf16[24,9344]{1,0:T(8,128)(2,1)S(1)}, bf16[24,9344]{1,0:T(8,128)(2,1)}, u32[]{:S(2)}) copy-start(bf16[24,9344]{1,0:T(8,128)(2,1)} %reduce-scatter.4.cloned.1.call-done) | copy-start | bytes 1345540
Sparse Core Ops, SparseCore 0:
  10.3 52.2 all-gather.3
  64.9 41.7 all-gather.5
  109.0 58.7 all-gather.7
  264.5 160.2 reduce-scatter.3
